TPU v7x, 32 devices: a whole 2x2x4 slice. The times are simulated.
32 devices in a mesh: groups: 2 (over y), attn: 4 (over x, core), exp: 4 (over z).
Axes of the slice: x: 2, y: 2, z: 4, core: 2. Of those that a mesh axis runs over, the one named last changes fastest.
Arguments:
- queries: bfloat16 [64, 32, 4096], P(('groups', 'exp'), None, 'attn'), parts along dimension 0, may hold values from -20 to 20
- new_keys: bfloat16 [64, 32, 512], P(('groups', 'exp'), None, 'attn'), parts along dimension 0, may hold values from -4 to 4
- new_values: bfloat16 [64, 32, 512], P(('groups', 'exp'), None, 'attn'), parts along dimension 0, may hold values from -4 to 4
- cache_keys: bfloat16 [64, 256, 512], P(('groups', 'exp'), None, 'attn'), parts along dimension 0, may hold values from -4 to 4
- cache_values: bfloat16 [64, 256, 512], P(('groups', 'exp'), None, 'attn'), parts along dimension 0, may hold values from -4 to 4
- cache_len: int32 [64], P(('groups', 'exp')), parts along dimension 0, may hold values from 2 to 256, as said below
- out_weight: bfloat16 [4096, 2048], P('attn', 'exp'), may hold values from -4 to 4
- residual: float32 [2048, 2048], P(('groups', 'exp', 'attn')), parts along dimension 0, may hold values from -6 to 6
- norm_gain: float32 [2048], replicated, may hold values from 0.1 to 1.9
- expert_ids: int32 [2048, 8], P(('groups', 'exp', 'attn')), parts along dimension 0, may hold values from 0 to 15, all different within a row; in each aligned block of 64 rows (0 to 63, 64 to 127, ...) at most 64 rows name the same one
- gate_nums: int32 [2048, 8], P(('groups', 'exp', 'attn')), parts along dimension 0, may hold values from 1 to 16
- w_gate_up: bfloat16 [16, 2048, 1536], P(('attn', 'exp')), may hold values from -0.125 to 0.125
- w_down: bfloat16 [16, 768, 2048], P(('attn', 'exp')), may hold values from -0.21875 to 0.21875
Outputs:
- mixed: float32 [2048, 2048], P(('groups', 'exp', 'attn')), parts along dimension 0
There are 2 independent parts, one for each index of `groups`. A program takes and returns all parts, laid end to end along the dimension named above; an argument that names none is the same for every part. Nothing has to cross between parts.
Inputs may be any that keep to these rules, and one draw needn't show every extreme that they name: `cache_len`: number of valid cache slots of each session; some session has all 256. `expert_ids`: within the 64 rows of one device, no expert is named by more than 64 rows, and this bound is reached; each row names 8 distinct experts.
All inputs are finite; a program needn't handle non-finite values.
Results may differ from a plain program's by a relative error of at most 0.0038.
Values may be sent and summed in bfloat16 or wider, within the bound.
A program may use at most 128 MiB of HBM per device.

v0:
```python
import jax
import jax.numpy as jnp
from jax import lax
from jax.sharding import PartitionSpec as P

HD = 128


def attend_session(packed):
    q_s, k_new, v_new, k_old, v_old, length = packed
    n_new = q_s.shape[0]
    n_old = k_old.shape[0]
    kv_count = k_old.shape[-1] // HD
    group_size = q_s.shape[-1] // (kv_count * HD)
    q_four = q_s.reshape(n_new, kv_count, group_size, HD)
    k_old3 = k_old.reshape(n_old, kv_count, HD)
    v_old3 = v_old.reshape(n_old, kv_count, HD)
    k_new3 = k_new.reshape(n_new, kv_count, HD)
    v_new3 = v_new.reshape(n_new, kv_count, HD)
    scale = 1.0 / HD**0.5
    s_old = jnp.einsum("ikgd,jkd->kgij", q_four, k_old3, preferred_element_type=jnp.float32) * scale
    s_new = jnp.einsum("ikgd,jkd->kgij", q_four, k_new3, preferred_element_type=jnp.float32) * scale
    valid_old = jnp.arange(n_old, dtype=jnp.int32) < length
    s_old = jnp.where(valid_old[None, None, None, :], s_old, jnp.float32(-1e30))
    causal = (
        jnp.arange(n_new, dtype=jnp.int32)[None, :] <= jnp.arange(n_new, dtype=jnp.int32)[:, None]
    )
    s_new = jnp.where(causal[None, None], s_new, jnp.float32(-1e30))
    top = jnp.maximum(jnp.max(s_old, -1, keepdims=True), jnp.max(s_new, -1, keepdims=True))
    e_old = jnp.exp(s_old - top)
    e_new = jnp.exp(s_new - top)
    total = jnp.sum(e_old, -1, keepdims=True) + jnp.sum(e_new, -1, keepdims=True)
    p_old = (e_old / total).astype(jnp.bfloat16)
    p_new = (e_new / total).astype(jnp.bfloat16)
    out = jnp.einsum("kgij,jkd->ikgd", p_old, v_old3, preferred_element_type=jnp.float32)
    out = out + jnp.einsum("kgij,jkd->ikgd", p_new, v_new3, preferred_element_type=jnp.float32)
    return out.reshape(n_new, kv_count * group_size * HD).astype(jnp.bfloat16)


def shards(
    queries,
    new_keys,
    new_values,
    cache_keys,
    cache_values,
    cache_len,
    out_weight,
    residual,
    norm_gain,
    expert_ids,
    gate_nums,
    w_gate_up,
    w_down,
):
    attended = lax.map(
        attend_session, (queries, new_keys, new_values, cache_keys, cache_values, cache_len)
    )
    local_rows = attended.reshape(attended.shape[0] * attended.shape[1], attended.shape[2])
    spread = jnp.dot(
        lax.all_gather(local_rows, "exp", axis=0, tiled=True),
        out_weight,
        preferred_element_type=jnp.float32,
    )
    partial_value = lax.all_to_all(spread, "exp", split_axis=0, concat_axis=1, tiled=True)
    projected = lax.psum_scatter(partial_value, "attn", scatter_dimension=0, tiled=True)
    middle = residual + projected
    meansq = jnp.mean(middle * middle, -1, keepdims=True)
    normed = (middle * lax.rsqrt(meansq + 1e-06) * norm_gain).astype(jnp.bfloat16)
    tok_rows = expert_ids.shape[0]
    top_count = expert_ids.shape[1]
    exp_dev = w_gate_up.shape[0]
    hidden_units = w_down.shape[1]
    n_experts = exp_dev * lax.axis_size("attn") * lax.axis_size("exp")
    capacity = max(2, 2 * tok_rows * top_count // n_experts)
    flat_ids = expert_ids.reshape(-1)
    onehot = (flat_ids[:, None] == jnp.arange(n_experts, dtype=jnp.int32)[None, :]).astype(
        jnp.int32
    )
    before = jnp.cumsum(onehot, axis=0) - onehot
    slot = jnp.sum(before * onehot, -1)
    target = (flat_ids * capacity + slot).reshape(tok_rows, top_count)
    places = jnp.arange(n_experts * capacity, dtype=jnp.int32)
    placing = jnp.sum((places[:, None, None] == target[None, :, :]).astype(jnp.int32), -1).astype(
        jnp.bfloat16
    )
    sent = jnp.dot(placing, normed, preferred_element_type=jnp.float32).astype(jnp.bfloat16)
    sent = sent.reshape(n_experts, capacity, normed.shape[1])
    block = lax.all_to_all(sent, ("attn", "exp"), split_axis=0, concat_axis=0, tiled=True)
    n_src = block.shape[0] // exp_dev
    rows_four = block.reshape(n_src, exp_dev, block.shape[1], block.shape[2])
    both = jnp.einsum("sjmd,jdf->sjmf", rows_four, w_gate_up, preferred_element_type=jnp.float32)
    hidden = (jax.nn.silu(both[..., :hidden_units]) * both[..., hidden_units:]).astype(jnp.bfloat16)
    result = jnp.einsum("sjmf,jfd->sjmd", hidden, w_down, preferred_element_type=jnp.float32)
    result = result.astype(jnp.bfloat16).reshape(block.shape)
    returned = lax.all_to_all(result, ("attn", "exp"), split_axis=0, concat_axis=0, tiled=True)
    picked = (
        returned[flat_ids, slot].reshape(tok_rows, top_count, normed.shape[1]).astype(jnp.float32)
    )
    numer = gate_nums.astype(jnp.float32)
    weights = numer / jnp.sum(numer, -1, keepdims=True)
    return middle + jnp.sum(picked * weights[:, :, None], 1)


def solution(mesh):
    in_specs = (
        P(("groups", "exp"), None, "attn"),
        P(("groups", "exp"), None, "attn"),
        P(("groups", "exp"), None, "attn"),
        P(("groups", "exp"), None, "attn"),
        P(("groups", "exp"), None, "attn"),
        P(("groups", "exp")),
        P("attn", "exp"),
        P(("groups", "exp", "attn"), None),
        P(),
        P(("groups", "exp", "attn"), None),
        P(("groups", "exp", "attn"), None),
        P(("attn", "exp"), None, None),
        P(("attn", "exp"), None, None),
    )
    out_specs = P(("groups", "exp", "attn"), None)
    return jax.shard_map(shards, mesh=mesh, in_specs=in_specs, out_specs=out_specs, check_vma=False)
```

profile of v0, /device:TPU:0, one launch (start us, length us, event | category | flops | bytes accessed | tf_op | source)
XLA Modules:
  0.0 444.1 jit_solution(16870406145571783817)
XLA Ops:
  6.5 63.9 %while.10 = (s32[]{:T(128)}, bf16[8,32,1024]{2,1,0:T(8,128)(2,1)}, bf16[8,256,128]{2,1,0:T(8,128)(2,1)}, s32[8]{0:T(128)}, bf16[8,256,128]{2,1,0:T(8,128)(2,1)},...) while((s32[]{:T(128)}, bf16[8,32,1024]{2,1,0:T(8,128)(2,1)}, ...), condition=%wide.region_5.6_spmd, body=%wide.region_0.5_spmd.sunk | while | flops 38404864 | bytes 2165389 | solution.py:55
  6.5 1.5 dynamic_slice.54
  10.5 1.1 fusion.72
  14.7 1.3 dynamic_slice.54
  18.5 1.1 fusion.72
  22.6 1.3 dynamic_slice.54
  30.6 1.3 dynamic_slice.54
  34.4 1.1 fusion.72
  38.6 1.3 dynamic_slice.54
  42.4 1.1 fusion.72
  46.6 1.3 dynamic_slice.54
  50.4 1.1 fusion.72
  54.5 1.3 dynamic_slice.54
  58.4 1.1 fusion.72
  62.5 1.3 dynamic_slice.54
  66.3 1.1 fusion.72
  70.6 48.7 %all-gather.2.cloned.1.call-done = bf16[1024,1024]{1,0:T(8,128)(2,1)} async-done(((bf16[256,1024]{1,0:T(8,128)(2,1)}), bf16[1024,1024]{1,0:T(8,128)(2,1)}) %all-gather.2.cloned.1.call-update) | async-done | bytes 2097168 | tf_op jit(solution)/shard_map/all_gather | solution.py:60
  119.3 3.1 fusion.53
  122.4 50.9 %all_to_all.29 = f32[4,256,512]{2,1,0:T(8,128)S(1)} all-to-all(f32[4,256,512]{2,1,0:T(8,128)S(1)} %bitcast.131), channel_id=1, replica_groups=mesh['groups'=2,'attn'=4,'exp'=4] {'exp'}, dimensions={0} | all-to-all | bytes 4194304 | tf_op jit(solution)/shard_map/all_to_all | solution.py:64
  173.3 1.6 copy.56
  175.2 1.2 reduce-window.6
  177.7 27.8 %reduce-scatter.2.cloned.1.call-done = f32[64,2048]{1,0:T(8,128)} async-done(((f32[256,2048]{1,0:T(8,128)}), f32[64,2048]{1,0:T(8,128)}) %reduce-scatter.2.cloned.1.call-update) | async-done | bytes 524304 | tf_op jit(solution)/shard_map/reduce_scatter | solution.py:65
  205.5 1.4 multiply_reduce_fusion
  207.7 1.3 convolution_convert_fusion.1
  209.0 99.1 %all_to_all.30 = bf16[16,64,2048]{2,1,0:T(8,128)(2,1)S(1)} all-to-all(bf16[16,64,2048]{2,1,0:T(8,128)(2,1)S(1)} %bitcast.126), channel_id=1, replica_groups=mesh['groups'=2,'attn'=4,'exp'=4] {'attn','exp'}, dimensions={0} | all-to-all | bytes 8388608 | tf_op jit(solution)/shard_map/all_to_all | solution.py:88
  308.2 6.6 %fusion.30 = f32[16,1,64,1536]{3,2,0,1:T(8,128)S(1)} fusion(bf16[16,64,2048]{2,1,0:T(8,128)(2,1)S(1)} %all_to_all.30, bf16[1,2048,1536]{2,1,0:T(8,128)(2,1)S(1)} %bitcast.135), kind=kOutput, calls=%fused_computation.42 | convolution fusion | flops 6442450944 | bytes 16777216 | tf_op jit(solution)/shard_map/sjmd,jdf->sjmf/dot_general | solution.py:91
  314.8 5.1 %convolution_convert_fusion = bf16[16,64,2048]{2,1,0:T(8,128)(2,1)} fusion(bf16[1,768,2048]{2,1,0:T(8,128)(2,1)S(1)} %copy-done, f32[16,1,64,1536]{3,2,0,1:T(8,128)S(1)} %fusion.30), kind=kOutput, calls=%fused_computation.45 | convolution fusion | flops 3228041216 | bytes 13631488 | tf_op jit(solution)/shard_map/sjmf,jfd->sjmd/dot_general | solution.py:93
  319.9 4.8 %all-to-all-start.2 = ((bf16[16,64,2048]{2,1,0:T(8,128)(2,1)}), bf16[16,64,2048]{2,1,0:T(8,128)(2,1)}, u32[]{:S(2)}, u32[]{:S(2)}) async-start(bf16[16,64,2048]{2,1,0:T(8,128)(2,1)} %convolution_convert_fusion), calls=%async_computation.3 | async-start | bytes 8388608 | tf_op jit(solution)/shard_map/all_to_all | solution.py:95
  325.0 94.0 %all-to-all-done.2 = bf16[16,64,2048]{2,1,0:T(8,128)(2,1)} async-done(((bf16[16,64,2048]{2,1,0:T(8,128)(2,1)}), bf16[16,64,2048]{2,1,0:T(8,128)(2,1)}, u32[]{:S(2)}, u32[]{:S(2)}) %all-to-all-start.2) | async-done | bytes 4194336 | tf_op jit(solution)/shard_map/all_to_all | solution.py:95
  418.9 13.0 %gather_fusion = bf16[512,2048]{1,0:T(8,128)(2,1)} fusion(bf16[16,64,2048]{2,1,0:T(8,128)(2,1)} %all-to-all-done.2, s32[512]{0:T(512)S(1)} %bitcast.125), kind=kCustom, calls=%fused_computation | custom fusion | bytes 4198400 | tf_op jit(solution)/shard_map/gather | solution.py:97
  431.9 3.4 fusion.33
  435.4 1.9 add.75
  (152 shorter events, 47.5 us)
Async XLA Ops:
  6.5 308.3 %copy-start = (bf16[1,768,2048]{2,1,0:T(8,128)(2,1)S(1)}, bf16[1,768,2048]{2,1,0:T(8,128)(2,1)}, u32[]{:S(2)}) copy-start(bf16[1,768,2048]{2,1,0:T(8,128)(2,1)} %param.27) | copy-start | bytes 9437188
  6.5 112.8 %all-gather.2.cloned.1.call-start = ((), (), s32[]{:S(2)}) async-start(), calls=%async_computation.4 | async-start | bytes 2621440 | tf_op jit(solution)/shard_map/all_gather | solution.py:60
  70.5 135.0 %reduce-scatter.2.cloned.1.call-start = ((), (), s32[]{:S(2)}) async-start(), calls=%async_computation.5 | async-start | bytes 2621440 | tf_op jit(solution)/shard_map/reduce_scatter | solution.py:65
  173.3 1.6 copy-start.2
  174.9 32.8 %copy-start.4 = (f32[2048]{0:T(1024)S(1)}, f32[2048]{0:T(1024)}, u32[]{:S(2)}) copy-start(f32[2048]{0:T(1024)} %param.23) | copy-start | bytes 24580
  206.9 0.8 copy-start.1
  207.7 100.5 %slice-start = ((s8[6291456]{0:T(1024)(128)(4,1)}), s8[4194304]{0:T(1024)(128)(4,1)S(1)}, s32[]{:S(2)}) async-start(s8[6291456]{0:T(1024)(128)(4,1)} %bitcast.134), calls=%async_computation.6 | async-start | bytes 8388608
  209.0 99.1 %slice-start.1 = ((s8[6291456]{0:T(1024)(128)(4,1)}), s8[2097152]{0:T(1024)(128)(4,1)S(1)}, s32[]{:S(2)}) async-start(s8[6291456]{0:T(1024)(128)(4,1)} %bitcast.134), calls=%async_computation.7 | async-start | bytes 4194304
  319.9 4.9 %copy-start.3 = (s32[64,8]{0,1:T(8,128)S(1)}, s32[64,8]{0,1:T(8,128)}, u32[]{:S(2)}) copy-start(s32[64,8]{0,1:T(8,128)} %param.25) | copy-start | bytes 6148
  319.9 99.0 %all-to-all-start.2 = ((bf16[16,64,2048]{2,1,0:T(8,128)(2,1)}), bf16[16,64,2048]{2,1,0:T(8,128)(2,1)}, u32[]{:S(2)}, u32[]{:S(2)}) async-start(bf16[16,64,2048]{2,1,0:T(8,128)(2,1)} %convolution_convert_fusion), calls=%async_computation.3 | async-start | bytes 8388608 | tf_op jit(solution)/shard_map/all_to_all | solution.py:95
Sparse Core Ops, SparseCore 0:
  70.6 48.6 all-gather.1
  175.1 30.4 reduce-scatter.1
where the time goes:
time: 447 us; the launch traced here: 444 us
  waiting for transfers between devices  171 us (38%)
  blocking collectives  150 us (34%)
  matrix products  48.7 us (11%)
  local copies, waits for them, and re-layouts  39.5 us (9%)
  other arithmetic  16.3 us (4%)
  between operations  13.5 us (3%)
  starting transfers between devices  4.89 us (1%)
    all_to_all x1, blocking collectives, shards(): lax.all_to_all(sent, ('attn', 'exp'), split_axis=0, concat_axis=0, tiled=...  99.1 us
    all_to_all x1, waiting for transfers between devices, shards(): lax.all_to_all(result, ('attn', 'exp'), split_axis=0, concat_axis=0, tile...  94 us
    all_to_all x1, blocking collectives, shards(): lax.all_to_all(spread, 'exp', split_axis=0, concat_axis=1, tiled=True)  50.9 us
    all_gather x1, waiting for transfers between devices, shards(): lax.all_gather(local_rows, 'exp', axis=0, tiled=True)  48.7 us
    reduce_scatter x1, waiting for transfers between devices, shards(): lax.psum_scatter(partial_value, 'attn', scatter_dimension=0, tiled=True)  27.8 us
    gather x1, local copies, waits for them, and re-layouts, shards(): returned[flat_ids, slot].reshape(tok_rows, top_count, normed.shape[1])  13 us
    dynamic_slice x8, local copies, waits for them, and re-layouts, shards(): lax.map(attend_session, (queries, new_keys, new_values, cache_keys, cache...  10.7 us
  transfers between devices with their start and end apart: 3, of which 3 were waited for; matrix products, arithmetic and copies ran while one was open for 1% of the time, Pallas kernels for 0%

commit v1 on v0

--- a/solution.py
+++ b/solution.py
@@ -4,6 +4,28 @@
 from jax.sharding import PartitionSpec as P
 
 HD = 128
+
+
+def cut_along(array, dim, count):
+    before, after = (array.shape[:dim], array.shape[dim + 1 :])
+    return jnp.moveaxis(array.reshape(*before, count, -1, *after), dim, 0)
+
+
+def joined_along(tiles, dim):
+    tiles = jnp.moveaxis(tiles, 0, dim)
+    shape = tiles.shape
+    return tiles.reshape(*shape[:dim], shape[dim] * shape[dim + 1], *shape[dim + 2 :])
+
+
+def swapped_with_each(x, axis, split_dim, concat_dim):
+    devices, mine = (lax.axis_size(axis), lax.axis_index(axis))
+    blocks = cut_along(x, split_dim, devices)
+    outs = [blocks[mine]]
+    for step in range(1, devices):
+        sent = blocks[mine ^ step]
+        outs.append(lax.ppermute(sent, axis, [(i, i ^ step) for i in range(devices)]))
+    blocks = jnp.stack(outs)[mine ^ jnp.arange(devices)]
+    return joined_along(blocks, concat_dim)
 
 
 def attend_session(packed):
@@ -85,7 +107,7 @@
     )
     sent = jnp.dot(placing, normed, preferred_element_type=jnp.float32).astype(jnp.bfloat16)
     sent = sent.reshape(n_experts, capacity, normed.shape[1])
-    block = lax.all_to_all(sent, ("attn", "exp"), split_axis=0, concat_axis=0, tiled=True)
+    block = swapped_with_each(sent, ("attn", "exp"), 0, 0)
     n_src = block.shape[0] // exp_dev
     rows_four = block.reshape(n_src, exp_dev, block.shape[1], block.shape[2])
     both = jnp.einsum("sjmd,jdf->sjmf", rows_four, w_gate_up, preferred_element_type=jnp.float32)

time: 447 us -> 454 us (1.016)
  blocking collectives: 150 us -> 50.9 us
  starting transfers between devices: 4.89 us -> 52 us
  waiting for transfers between devices: 171 us -> 210 us
  local copies, waits for them, and re-layouts: 39.5 us -> 56.7 us
    all_to_all x1 -> x0, blocking collectives: 99.1 us -> none  [shards(): lax.all_to_all(sent, ('attn', 'exp'), split_axis=0, concat_axis=0, tiled=...]
    ppermute x0 -> x15, starting transfers between devices: none -> 41.4 us  [swapped_with_each(): lax.ppermute(sent, axis, [(i, i ^ step) for i in range(devices)])]
    ppermute x0 -> x15, waiting for transfers between devices: none -> 39 us  [swapped_with_each(): lax.ppermute(sent, axis, [(i, i ^ step) for i in range(devices)])]
    unnamed x15 -> x25, local copies, waits for them, and re-layouts: 0.89 us -> 11.1 us
    all_to_all x1, starting transfers between devices: 4.85 us -> 10.6 us  [shards(): lax.all_to_all(result, ('attn', 'exp'), split_axis=0, concat_axis=0, tile...]
    gather x0 -> x1, local copies, waits for them, and re-layouts: none -> 4.97 us  [swapped_with_each(): blocks = jnp.stack(outs)[mine ^ jnp.arange(devices)]]
  transfers between devices with their start and end apart: 3 -> 18, of which waited for: 3 -> 9; matrix products, arithmetic and copies ran while one was open for 1% -> 3% of each run, Pallas kernels for 0% -> 0%
where the time goes in v1:
time: 454 us; the launch traced here: 452 us
  waiting for transfers between devices  210 us (46%)
  local copies, waits for them, and re-layouts  56.7 us (12%)
  starting transfers between devices  52 us (11%)
  matrix products  52 us (11%)
  blocking collectives  50.9 us (11%)
  other arithmetic  16.3 us (4%)
  between operations  13.6 us (3%)
    all_to_all x1, waiting for transfers between devices, shards(): lax.all_to_all(result, ('attn', 'exp'), split_axis=0, concat_axis=0, tile...  94.2 us
    all_to_all x1, blocking collectives, shards(): lax.all_to_all(spread, 'exp', split_axis=0, concat_axis=1, tiled=True)  50.9 us
    all_gather x1, waiting for transfers between devices, shards(): lax.all_gather(local_rows, 'exp', axis=0, tiled=True)  48.7 us
    ppermute x15, starting transfers between devices, swapped_with_each(): lax.ppermute(sent, axis, [(i, i ^ step) for i in range(devices)])  41.4 us
    ppermute x15, waiting for transfers between devices, swapped_with_each(): lax.ppermute(sent, axis, [(i, i ^ step) for i in range(devices)])  39 us
    reduce_scatter x1, waiting for transfers between devices, shards(): lax.psum_scatter(partial_value, 'attn', scatter_dimension=0, tiled=True)  27.8 us
    gather x1, local copies, waits for them, and re-layouts, shards(): returned[flat_ids, slot].reshape(tok_rows, top_count, normed.shape[1])  13 us
    unnamed x25, local copies, waits for them, and re-layouts  11.1 us
  transfers between devices with their start and end apart: 18, of which 9 were waited for; matrix products, arithmetic and copies ran while one was open for 3% of the time, Pallas kernels for 0%

profile of v1, /device:TPU:0, one launch (start us, length us, event | category | flops | bytes accessed | tf_op | source)
XLA Modules:
  0.0 452.0 jit_solution(15842743970440035173)
XLA Ops:
  6.5 63.9 %while.10 = (s32[]{:T(128)}, bf16[8,32,1024]{2,1,0:T(8,128)(2,1)}, bf16[8,256,128]{2,1,0:T(8,128)(2,1)}, s32[8]{0:T(128)}, bf16[8,256,128]{2,1,0:T(8,128)(2,1)},...) while((s32[]{:T(128)}, bf16[8,32,1024]{2,1,0:T(8,128)(2,1)}, ...), condition=%wide.region_5.6_spmd, body=%wide.region_0.5_spmd.sunk | while | flops 38404864 | bytes 2167921 | solution.py:77
  7.6 1.3 dynamic_slice.134
  15.5 1.3 dynamic_slice.134
  23.5 1.3 dynamic_slice.134
  31.5 1.3 dynamic_slice.134
  39.4 1.3 dynamic_slice.134
  70.6 48.7 %all-gather.2.cloned.1.call-done = bf16[1024,1024]{1,0:T(8,128)(2,1)} async-done(((bf16[256,1024]{1,0:T(8,128)(2,1)}), bf16[1024,1024]{1,0:T(8,128)(2,1)}) %all-gather.2.cloned.1.call-update) | async-done | bytes 2097168 | tf_op jit(solution)/shard_map/all_gather | solution.py:82
  119.3 3.1 fusion.54
  122.4 50.9 %all_to_all.24 = f32[4,256,512]{2,1,0:T(8,128)S(1)} all-to-all(f32[4,256,512]{2,1,0:T(8,128)S(1)} %bitcast.194), channel_id=1, replica_groups=mesh['groups'=2,'attn'=4,'exp'=4] {'exp'}, dimensions={0} | all-to-all | bytes 4194304 | tf_op jit(solution)/shard_map/all_to_all | solution.py:86
  173.3 1.6 copy.56
  177.8 27.8 %reduce-scatter.2.cloned.1.call-done = f32[64,2048]{1,0:T(8,128)} async-done(((f32[256,2048]{1,0:T(8,128)}), f32[64,2048]{1,0:T(8,128)}) %reduce-scatter.2.cloned.1.call-update) | async-done | bytes 524304 | tf_op jit(solution)/shard_map/reduce_scatter | solution.py:87
  205.6 1.4 multiply_reduce_fusion
  209.1 1.3 dynamic-slice_bitcast_fusion.1
  210.4 1.5 collective-permute-start
  211.9 2.5 collective-permute-start.1
  215.6 8.8 %collective-permute-done = bf16[1,64,2048]{2,1,0:T(8,128)(2,1)S(1)} collective-permute-done((bf16[1,64,2048]{2,1,0:T(8,128)(2,1)S(1)}, bf16[1,64,2048]{2,1,0:T(8,128)(2,1)S(1)}, u32[]{:S(2)}, u32[]{:S(2)}) %collective-permute-start) | collective-permute-done | bytes 262176 | tf_op jit(solution)/shard_map/ppermute | solution.py:26
  225.1 8.3 %collective-permute-done.1 = bf16[1,64,2048]{2,1,0:T(8,128)(2,1)S(1)} collective-permute-done((bf16[1,64,2048]{2,1,0:T(8,128)(2,1)S(1)}, bf16[1,64,2048]{2,1,0:T(8,128)(2,1)S(1)}, u32[]{:S(2)}, u32[]{:S(2)}) %collective-permute-start.1) | collective-permute-done | bytes 262176 | tf_op jit(solution)/shard_map/ppermute | solution.py:26
  235.4 17.6 %collective-permute-start.8 = (bf16[1,64,2048]{2,1,0:T(8,128)(2,1)S(1)}, bf16[1,64,2048]{2,1,0:T(8,128)(2,1)S(1)}, u32[]{:S(2)}, u32[]{:S(2)}) collective-permute-start(bf16[1,64,2048]{2,1,0:T(8,128)(2,1)S(1)} %get-tuple-element.76), channel_id=1, source_target_pairs={{0,9},{1,8},{2,11},{3,10},{4,13},{5,12},{6,15},{7,14},{8,1},{9,0},... | collective-permute-start | bytes 786440 | tf_op jit(solution)/shard_map/ppermute | solution.py:26
  256.0 2.4 collective-permute-start.10
  259.1 3.7 collective-permute-start.11
  263.5 10.8 %collective-permute-start.12 = (bf16[1,64,2048]{2,1,0:T(8,128)(2,1)S(1)}, bf16[1,64,2048]{2,1,0:T(8,128)(2,1)S(1)}, u32[]{:S(2)}, u32[]{:S(2)}) collective-permute-start(bf16[1,64,2048]{2,1,0:T(8,128)(2,1)S(1)} %get-tuple-element.72), channel_id=1, source_target_pairs={{0,13},{1,12},{2,15},{3,14},{4,9},{5,8},{6,11},{7,10},{8,5},{9,4},... | collective-permute-start | bytes 786440 | tf_op jit(solution)/shard_map/ppermute | solution.py:26
  275.9 2.6 collective-permute-done.9
  280.0 8.4 %collective-permute-done.11 = bf16[1,64,2048]{2,1,0:T(8,128)(2,1)S(1)} collective-permute-done((bf16[1,64,2048]{2,1,0:T(8,128)(2,1)S(1)}, bf16[1,64,2048]{2,1,0:T(8,128)(2,1)S(1)}, u32[]{:S(2)}, u32[]{:S(2)}) %collective-permute-start.11) | collective-permute-done | bytes 262176 | tf_op jit(solution)/shard_map/ppermute | solution.py:26
  289.9 10.4 %collective-permute-done.13 = bf16[1,64,2048]{2,1,0:T(8,128)(2,1)S(1)} collective-permute-done((bf16[1,64,2048]{2,1,0:T(8,128)(2,1)S(1)}, bf16[1,64,2048]{2,1,0:T(8,128)(2,1)S(1)}, u32[]{:S(2)}, u32[]{:S(2)}) %collective-permute-start.13) | collective-permute-done | bytes 262176 | tf_op jit(solution)/shard_map/ppermute | solution.py:26
  301.8 5.0 %gather_fusion = bf16[16,64,2048]{2,1,0:T(8,128)(2,1)} fusion(bf16[16,64,2048]{2,1,0:T(8,128)(2,1)} %bitcast.52, s32[1024]{0:T(1024)S(1)} %pad_clamp_fusion), kind=kCustom, calls=%fused_computation | custom fusion | bytes 8388672 | tf_op jit(solution)/shard_map/gather | solution.py:27
  306.8 10.0 %fusion.30 = f32[16,1,64,1536]{3,2,0,1:T(8,128)S(1)} fusion(bf16[16,64,2048]{2,1,0:T(8,128)(2,1)} %gather_fusion, bf16[1,2048,1536]{2,1,0:T(8,128)(2,1)} %param.26), kind=kOutput, calls=%fused_computation.43 | convolution fusion | flops 6442450944 | bytes 16777216 | tf_op jit(solution)/shard_map/sjmd,jdf->sjmf/dot_general | solution.py:113
  316.8 5.0 %convolution_convert_fusion = bf16[16,64,2048]{2,1,0:T(8,128)(2,1)} fusion(bf16[1,768,2048]{2,1,0:T(8,128)(2,1)S(1)} %copy-done, f32[16,1,64,1536]{3,2,0,1:T(8,128)S(1)} %fusion.30), kind=kOutput, calls=%fused_computation.46 | convolution fusion | flops 3228041216 | bytes 13631488 | tf_op jit(solution)/shard_map/sjmf,jfd->sjmd/dot_general | solution.py:115
  321.8 10.6 %all-to-all-start.1 = ((bf16[16,64,2048]{2,1,0:T(8,128)(2,1)}), bf16[16,64,2048]{2,1,0:T(8,128)(2,1)}, u32[]{:S(2)}, u32[]{:S(2)}) async-start(bf16[16,64,2048]{2,1,0:T(8,128)(2,1)} %convolution_convert_fusion), calls=%async_computation.2 | async-start | bytes 8388608 | tf_op jit(solution)/shard_map/all_to_all | solution.py:117
  332.6 94.2 %all-to-all-done.1 = bf16[16,64,2048]{2,1,0:T(8,128)(2,1)} async-done(((bf16[16,64,2048]{2,1,0:T(8,128)(2,1)}), bf16[16,64,2048]{2,1,0:T(8,128)(2,1)}, u32[]{:S(2)}, u32[]{:S(2)}) %all-to-all-start.1) | async-done | bytes 4194336 | tf_op jit(solution)/shard_map/all_to_all | solution.py:117
  426.8 13.0 %gather_fusion.1 = bf16[512,2048]{1,0:T(8,128)(2,1)} fusion(bf16[16,64,2048]{2,1,0:T(8,128)(2,1)} %all-to-all-done.1, s32[512]{0:T(512)S(1)} %bitcast.188), kind=kCustom, calls=%fused_computation.1 | custom fusion | bytes 4198400 | tf_op jit(solution)/shard_map/gather | solution.py:119
  439.8 3.4 fusion.33
  443.3 1.9 add.154
  (195 shorter events, 76.2 us)
Async XLA Ops:
  6.5 310.2 %copy-start = (bf16[1,768,2048]{2,1,0:T(8,128)(2,1)S(1)}, bf16[1,768,2048]{2,1,0:T(8,128)(2,1)}, u32[]{:S(2)}) copy-start(bf16[1,768,2048]{2,1,0:T(8,128)(2,1)} %param.27) | copy-start | bytes 9437188
  6.5 112.8 %all-gather.2.cloned.1.call-start = ((), (), s32[]{:S(2)}) async-start(), calls=%async_computation.3 | async-start | bytes 2621440 | tf_op jit(solution)/shard_map/all_gather | solution.py:82
  70.5 135.1 %reduce-scatter.2.cloned.1.call-start = ((), (), s32[]{:S(2)}) async-start(), calls=%async_computation.4 | async-start | bytes 2621440 | tf_op jit(solution)/shard_map/reduce_scatter | solution.py:87
  173.3 1.7 copy-start.2
  173.3 34.4 %copy-start.4 = (f32[2048]{0:T(1024)S(1)}, f32[2048]{0:T(1024)}, u32[]{:S(2)}) copy-start(f32[2048]{0:T(1024)} %param.23) | copy-start | bytes 24580
  207.0 0.8 copy-start.1
  210.4 14.0 %collective-permute-start = (bf16[1,64,2048]{2,1,0:T(8,128)(2,1)S(1)}, bf16[1,64,2048]{2,1,0:T(8,128)(2,1)S(1)}, u32[]{:S(2)}, u32[]{:S(2)}) collective-permute-start(bf16[1,64,2048]{2,1,0:T(8,128)(2,1)S(1)} %get-tuple-element.84), channel_id=1, source_target_pairs={{0,1},{1,0},{2,3},{3,2},{4,5},{5,4},{6,7},{7,6},{8,9},{9,8},{10,11... | collective-permute-start | bytes 786440 | tf_op jit(solution)/shard_map/ppermute | solution.py:26
  211.9 21.5 %collective-permute-start.1 = (bf16[1,64,2048]{2,1,0:T(8,128)(2,1)S(1)}, bf16[1,64,2048]{2,1,0:T(8,128)(2,1)S(1)}, u32[]{:S(2)}, u32[]{:S(2)}) collective-permute-start(bf16[1,64,2048]{2,1,0:T(8,128)(2,1)S(1)} %get-tuple-element.83), channel_id=1, source_target_pairs={{0,2},{1,3},{2,0},{3,1},{4,6},{5,7},{6,4},{7,5},{8,10},{9,11},{10,... | collective-permute-start | bytes 786440 | tf_op jit(solution)/shard_map/ppermute | solution.py:26
  214.4 19.7 %collective-permute-start.2 = (bf16[1,64,2048]{2,1,0:T(8,128)(2,1)S(1)}, bf16[1,64,2048]{2,1,0:T(8,128)(2,1)S(1)}, u32[]{:S(2)}, u32[]{:S(2)}) collective-permute-start(bf16[1,64,2048]{2,1,0:T(8,128)(2,1)S(1)} %get-tuple-element.82), channel_id=1, source_target_pairs={{0,3},{1,2},{2,1},{3,0},{4,7},{5,6},{6,5},{7,4},{8,11},{9,10},{10,... | collective-permute-start | bytes 786440 | tf_op jit(solution)/shard_map/ppermute | solution.py:26
  214.9 20.5 %collective-permute-start.3 = (bf16[1,64,2048]{2,1,0:T(8,128)(2,1)S(1)}, bf16[1,64,2048]{2,1,0:T(8,128)(2,1)S(1)}, u32[]{:S(2)}, u32[]{:S(2)}) collective-permute-start(bf16[1,64,2048]{2,1,0:T(8,128)(2,1)S(1)} %get-tuple-element.81), channel_id=1, source_target_pairs={{0,4},{1,5},{2,6},{3,7},{4,0},{5,1},{6,2},{7,3},{8,12},{9,13},{10,... | collective-permute-start | bytes 786440 | tf_op jit(solution)/shard_map/ppermute | solution.py:26
  214.9 38.9 %collective-permute-start.4 = (bf16[1,64,2048]{2,1,0:T(8,128)(2,1)S(1)}, bf16[1,64,2048]{2,1,0:T(8,128)(2,1)S(1)}, u32[]{:S(2)}, u32[]{:S(2)}) collective-permute-start(bf16[1,64,2048]{2,1,0:T(8,128)(2,1)S(1)} %get-tuple-element.80), channel_id=1, source_target_pairs={{0,5},{1,4},{2,7},{3,6},{4,1},{5,0},{6,3},{7,2},{8,13},{9,12},{10,... | collective-permute-start | bytes 786440 | tf_op jit(solution)/shard_map/ppermute | solution.py:26
  224.4 31.6 %collective-permute-start.5 = (bf16[1,64,2048]{2,1,0:T(8,128)(2,1)S(1)}, bf16[1,64,2048]{2,1,0:T(8,128)(2,1)S(1)}, u32[]{:S(2)}, u32[]{:S(2)}) collective-permute-start(bf16[1,64,2048]{2,1,0:T(8,128)(2,1)S(1)} %get-tuple-element.79), channel_id=1, source_target_pairs={{0,6},{1,7},{2,4},{3,5},{4,2},{5,3},{6,0},{7,1},{8,14},{9,15},{10,... | collective-permute-start | bytes 786440 | tf_op jit(solution)/shard_map/ppermute | solution.py:26
  233.4 25.7 %collective-permute-start.6 = (bf16[1,64,2048]{2,1,0:T(8,128)(2,1)S(1)}, bf16[1,64,2048]{2,1,0:T(8,128)(2,1)S(1)}, u32[]{:S(2)}, u32[]{:S(2)}) collective-permute-start(bf16[1,64,2048]{2,1,0:T(8,128)(2,1)S(1)} %get-tuple-element.78), channel_id=1, source_target_pairs={{0,7},{1,6},{2,5},{3,4},{4,3},{5,2},{6,1},{7,0},{8,15},{9,14},{10,... | collective-permute-start | bytes 786440 | tf_op jit(solution)/shard_map/ppermute | solution.py:26
  234.1 29.4 %collective-permute-start.7 = (bf16[1,64,2048]{2,1,0:T(8,128)(2,1)S(1)}, bf16[1,64,2048]{2,1,0:T(8,128)(2,1)S(1)}, u32[]{:S(2)}, u32[]{:S(2)}) collective-permute-start(bf16[1,64,2048]{2,1,0:T(8,128)(2,1)S(1)} %get-tuple-element.77), channel_id=1, source_target_pairs={{0,8},{1,9},{2,10},{3,11},{4,12},{5,13},{6,14},{7,15},{8,0},{9,1},... | collective-permute-start | bytes 786440 | tf_op jit(solution)/shard_map/ppermute | solution.py:26
  235.4 39.6 %collective-permute-start.8 = (bf16[1,64,2048]{2,1,0:T(8,128)(2,1)S(1)}, bf16[1,64,2048]{2,1,0:T(8,128)(2,1)S(1)}, u32[]{:S(2)}, u32[]{:S(2)}) collective-permute-start(bf16[1,64,2048]{2,1,0:T(8,128)(2,1)S(1)} %get-tuple-element.76), channel_id=1, source_target_pairs={{0,9},{1,8},{2,11},{3,10},{4,13},{5,12},{6,15},{7,14},{8,1},{9,0},... | collective-permute-start | bytes 786440 | tf_op jit(solution)/shard_map/ppermute | solution.py:26
  253.8 24.6 %collective-permute-start.9 = (bf16[1,64,2048]{2,1,0:T(8,128)(2,1)S(1)}, bf16[1,64,2048]{2,1,0:T(8,128)(2,1)S(1)}, u32[]{:S(2)}, u32[]{:S(2)}) collective-permute-start(bf16[1,64,2048]{2,1,0:T(8,128)(2,1)S(1)} %get-tuple-element.75), channel_id=1, source_target_pairs={{0,10},{1,11},{2,8},{3,9},{4,14},{5,15},{6,12},{7,13},{8,2},{9,3},... | collective-permute-start | bytes 786440 | tf_op jit(solution)/shard_map/ppermute | solution.py:26
  256.0 23.3 %collective-permute-start.10 = (bf16[1,64,2048]{2,1,0:T(8,128)(2,1)S(1)}, bf16[1,64,2048]{2,1,0:T(8,128)(2,1)S(1)}, u32[]{:S(2)}, u32[]{:S(2)}) collective-permute-start(bf16[1,64,2048]{2,1,0:T(8,128)(2,1)S(1)} %get-tuple-element.74), channel_id=1, source_target_pairs={{0,11},{1,10},{2,9},{3,8},{4,15},{5,14},{6,13},{7,12},{8,3},{9,2},... | collective-permute-start | bytes 786440 | tf_op jit(solution)/shard_map/ppermute | solution.py:26
  259.1 29.4 %collective-permute-start.11 = (bf16[1,64,2048]{2,1,0:T(8,128)(2,1)S(1)}, bf16[1,64,2048]{2,1,0:T(8,128)(2,1)S(1)}, u32[]{:S(2)}, u32[]{:S(2)}) collective-permute-start(bf16[1,64,2048]{2,1,0:T(8,128)(2,1)S(1)} %get-tuple-element.73), channel_id=1, source_target_pairs={{0,12},{1,13},{2,14},{3,15},{4,8},{5,9},{6,10},{7,11},{8,4},{9,5},... | collective-permute-start | bytes 786440 | tf_op jit(solution)/shard_map/ppermute | solution.py:26
  263.5 25.7 %collective-permute-start.12 = (bf16[1,64,2048]{2,1,0:T(8,128)(2,1)S(1)}, bf16[1,64,2048]{2,1,0:T(8,128)(2,1)S(1)}, u32[]{:S(2)}, u32[]{:S(2)}) collective-permute-start(bf16[1,64,2048]{2,1,0:T(8,128)(2,1)S(1)} %get-tuple-element.72), channel_id=1, source_target_pairs={{0,13},{1,12},{2,15},{3,14},{4,9},{5,8},{6,11},{7,10},{8,5},{9,4},... | collective-permute-start | bytes 786440 | tf_op jit(solution)/shard_map/ppermute | solution.py:26
  275.0 25.3 %collective-permute-start.13 = (bf16[1,64,2048]{2,1,0:T(8,128)(2,1)S(1)}, bf16[1,64,2048]{2,1,0:T(8,128)(2,1)S(1)}, u32[]{:S(2)}, u32[]{:S(2)}) collective-permute-start(bf16[1,64,2048]{2,1,0:T(8,128)(2,1)S(1)} %get-tuple-element.71), channel_id=1, source_target_pairs={{0,14},{1,15},{2,12},{3,13},{4,10},{5,11},{6,8},{7,9},{8,6},{9,7},... | collective-permute-start | bytes 786440 | tf_op jit(solution)/shard_map/ppermute | solution.py:26
  278.4 22.6 %collective-permute-start.14 = (bf16[1,64,2048]{2,1,0:T(8,128)(2,1)S(1)}, bf16[1,64,2048]{2,1,0:T(8,128)(2,1)S(1)}, u32[]{:S(2)}, u32[]{:S(2)}) collective-permute-start(bf16[1,64,2048]{2,1,0:T(8,128)(2,1)S(1)} %get-tuple-element.70), channel_id=1, source_target_pairs={{0,15},{1,14},{2,13},{3,12},{4,11},{5,10},{6,9},{7,8},{8,7},{9,6},... | collective-permute-start | bytes 786440 | tf_op jit(solution)/shard_map/ppermute | solution.py:26
  321.8 10.7 %copy-start.3 = (s32[64,8]{0,1:T(8,128)S(1)}, s32[64,8]{0,1:T(8,128)}, u32[]{:S(2)}) copy-start(s32[64,8]{0,1:T(8,128)} %param.25) | copy-start | bytes 6148
  321.8 105.0 %all-to-all-start.1 = ((bf16[16,64,2048]{2,1,0:T(8,128)(2,1)}), bf16[16,64,2048]{2,1,0:T(8,128)(2,1)}, u32[]{:S(2)}, u32[]{:S(2)}) async-start(bf16[16,64,2048]{2,1,0:T(8,128)(2,1)} %convolution_convert_fusion), calls=%async_computation.2 | async-start | bytes 8388608 | tf_op jit(solution)/shard_map/all_to_all | solution.py:117
Sparse Core Ops, SparseCore 0:
  70.6 48.6 all-gather.1
  175.1 30.4 reduce-scatter.1
